TPU v7x, 128 devices: a whole 4x4x4 slice. The times are simulated.
128 devices in a mesh: section: 8 (over z_hi, y), seq: 8 (over x, z_lo), mp: 2 (over core).
Axes of the slice: x: 4, y: 4, z: 4 (z_hi: 2, z_lo: 2; z = z_hi * 2 + z_lo), core: 2. Of those that a mesh axis runs over, the one named last changes fastest.
Arguments:
- resid: bfloat16 [8, 2048, 4096], P('section', 'seq', 'mp'), may hold values from -3 to 3
- span_q: bfloat16 [8, 2048, 4096], P('section', 'seq', 'mp'), may hold values from -6 to 6
- span_k: bfloat16 [8, 2048, 4096], P('section', 'seq', 'mp'), may hold values from -6 to 6
- span_v: bfloat16 [8, 2048, 4096], P('section', 'seq', 'mp'), may hold values from -6 to 6
- cache_k: bfloat16 [4, 2048, 4096], P(None, 'seq', 'mp'), may hold values from -6 to 6
- cache_v: bfloat16 [4, 2048, 4096], P(None, 'seq', 'mp'), may hold values from -6 to 6
- cache_index: int32 [8], P('section'), may hold values from 0 to 3
- tile_mask: int32 [8, 16, 48], P('section'), may hold values from 0 to 1, as said below
Outputs:
- updated: bfloat16 [8, 2048, 4096], P('section', 'seq', 'mp')
Inputs may be any that keep to these rules, and one draw needn't show every extreme that they name: tile_mask[s, i, i] is 1 for every group s and query tile i: every query tile sees its own key tile.
All inputs are finite; a program needn't handle non-finite values.
Results may differ from a plain program's by a relative error of at most 0.0044.
Values may be sent and summed in bfloat16 or wider, within the bound.
A program may use at most 320 MiB of HBM per device.

v0:
```python
import math
import jax
import jax.numpy as jnp
from jax import lax
from jax.sharding import PartitionSpec as P

HD = 128
TILE = 128


def shifted(value, axis, steps):
    count = lax.axis_size(axis)
    first, last = (max(0, -steps), min(count, count - steps))
    return lax.ppermute(value, axis, [(source, source + steps) for source in range(first, last)])


def spread(block, axis, holder):
    block = jnp.where(lax.axis_index(axis) == holder, block, jnp.zeros_like(block))
    return lax.psum(block, axis)


def one_hot_rows(ids, count):
    return (ids[:, None] == jnp.arange(count)[None, :]).astype(jnp.float32)


def absorb(carry, queries, keys, values, allowed):
    top, total, acc = carry
    count = keys.shape[0]
    heads = queries.shape[1]
    key_heads = keys.reshape(count, heads, HD)
    value_heads = values.reshape(count, heads, HD)
    score = jnp.einsum("qhd,khd->hqk", queries, key_heads, preferred_element_type=jnp.float32) * (
        1.0 / math.sqrt(HD)
    )
    masked = jnp.where(allowed[None], score, -1e30)
    new_top = jnp.maximum(top, jnp.max(masked, axis=2))
    expo = jnp.where(allowed[None], jnp.exp(masked - new_top[:, :, None]), 0.0)
    factor = jnp.exp(top - new_top)
    total = total * factor + jnp.sum(expo, axis=2)
    mixed = jnp.einsum(
        "hqk,khd->qhd", expo.astype(jnp.bfloat16), value_heads, preferred_element_type=jnp.float32
    )
    acc = acc * factor.T[:, :, None] + mixed
    return (new_top, total, acc)


def body(resid, span_q, span_k, span_v, cache_k, cache_v, cache_index, tile_mask):
    incoming = shifted(resid, "section", 1)
    rows = span_q.shape[1]
    width = span_q.shape[2]
    heads = width // HD
    final_section = lax.axis_size("section") - 1
    query_tiles = tile_mask.shape[1]
    key_tiles = tile_mask.shape[2]
    mask_rows = tile_mask[0].astype(jnp.float32)
    cached_k = lax.dynamic_index_in_dim(cache_k, cache_index[0], 0, keepdims=False)
    cached_v = lax.dynamic_index_in_dim(cache_v, cache_index[0], 0, keepdims=False)
    fresh_k, fresh_v = (
        spread(span_k[0], "section", final_section),
        spread(span_v[0], "section", final_section),
    )
    first_row = lax.axis_index("seq") * rows
    query_ids = (first_row + jnp.arange(rows)) // TILE
    row_allow = jnp.dot(one_hot_rows(query_ids, query_tiles), mask_rows)
    queries = span_q[0].reshape(rows, heads, HD)
    init = (
        jnp.full((heads, rows), -1e30, jnp.float32),
        jnp.zeros((heads, rows), jnp.float32),
        jnp.zeros((rows, heads, HD), jnp.float32),
    )
    carry = init
    pieces = (
        lax.all_gather(span_k[0], "seq", axis=0, tiled=True),
        lax.all_gather(span_v[0], "seq", axis=0, tiled=True),
        lax.all_gather(fresh_k, "seq", axis=0, tiled=True),
        lax.all_gather(fresh_v, "seq", axis=0, tiled=True),
        lax.all_gather(cached_k, "seq", axis=0, tiled=True),
        lax.all_gather(cached_v, "seq", axis=0, tiled=True),
    )
    count = pieces[0].shape[0]
    for group in range(3):
        tiles = jnp.arange(count) // TILE + group * query_tiles
        allowed = jnp.dot(row_allow, one_hot_rows(tiles, key_tiles).T) > 0.5
        carry = absorb(carry, queries, pieces[2 * group], pieces[2 * group + 1], allowed)
    top, total, acc = carry
    attn = (acc / total.T[:, :, None]).reshape(rows, width).astype(jnp.bfloat16)
    attn = lax.optimization_barrier(attn)
    updated = (incoming[0].astype(jnp.float32) + attn.astype(jnp.float32)).astype(jnp.bfloat16)
    return updated[None]


def solution(mesh):
    placed = (
        P("section", "seq", "mp"),
        P("section", "seq", "mp"),
        P("section", "seq", "mp"),
        P("section", "seq", "mp"),
        P(None, "seq", "mp"),
        P(None, "seq", "mp"),
        P("section"),
        P("section", None, None),
    )
    return jax.shard_map(
        body, mesh=mesh, in_specs=placed, out_specs=P("section", "seq", "mp"), check_vma=False
    )
```

profile of v0, /device:TPU:15, one launch (start us, length us, event | category | flops | bytes accessed | tf_op | source)
XLA Modules:
  0.0 1183.9 jit_solution(3314172403509252847)
XLA Ops:
  7.4 0.0 all-reduce.3.cloned.1.call-start
  7.4 1.5 copy.18
  8.9 0.0 copy-start
  8.9 1.9 copy.26
  10.7 1.1 select_bitcast_fusion.1
  11.8 1.1 select_bitcast_fusion
  12.9 0.0 all-reduce.3.cloned.1.call-update
  12.9 0.0 all-gather.21.cloned.1.call-start
  13.6 2.3 constant_dynamic-slice_fusion
  15.9 0.0 all-gather.21.cloned.1.call-update
  15.9 0.0 all-gather.17.cloned.1.call-start
  16.0 0.5 all-gather.17.cloned.1.call-update
  16.5 0.0 all-gather.19.cloned.1.call-start
  16.6 1.3 constant_dynamic-slice_fusion.1
  17.9 1.3 copy.38
  19.2 0.0 all-gather.19.cloned.1.call-update
  19.2 0.0 all-gather.15.cloned.1.call-start
  19.3 0.0 copy-done
  19.3 0.7 all-gather.15.cloned.1.call-update
  19.9 0.0 all-gather.11.cloned.1.call-start
  20.0 94.3 %all-reduce.3.cloned.1.call-done = (bf16[256,2048]{0,1:T(8,128)(2,1)}, bf16[256,2048]{0,1:T(8,128)(2,1)}) async-done(((bf16[256,2048]{0,1:T(8,128)(2,1)}, bf16[256,2048]{0,1:T(8,128)(2,1)}), (bf16[256,2048]{0,1:T(8,128)(2,1)}, bf16[256,2048]{0,1:T(8,128)(2,1)})) %all-reduce.3.cloned.1.call-update) | async-done | bytes 2097168 | tf_op jit(solution)/shard_map/psum | solution.py:19
  114.3 0.0 all-gather.11.cloned.1.call-update
  114.3 0.0 all-gather.13.cloned.1.call-start
  114.4 3.8 collective-permute-start
  118.2 0.0 all-gather.13.cloned.1.call-update
  118.2 1.5 copy.39
  119.7 0.9 fusion.35
  120.7 1.0 convolution_compare_fusion
  121.6 1.0 convolution_compare_fusion.1
  122.6 1.0 convolution_compare_fusion.2
  123.5 65.2 %all-gather.21.cloned.1.call-done = bf16[1,2048,2048]{2,1,0:T(8,128)(2,1)} async-done(((bf16[1,256,2048]{2,1,0:T(8,128)(2,1)}), bf16[1,2048,2048]{2,1,0:T(8,128)(2,1)}) %all-gather.21.cloned.1.call-update) | async-done | bytes 8388624 | tf_op jit(solution)/shard_map/all_gather | solution.py:78
  188.7 12.3 %copy.31 = bf16[1,2048,2048]{1,2,0:T(8,128)(2,1)} copy(bf16[1,2048,2048]{2,1,0:T(8,128)(2,1)} %all-gather.21.cloned.1.call-done) | data formatting | bytes 16777216 | tf_op jit(solution)/shard_map/all_gather | solution.py:78
  201.0 219.5 %all-gather.17.cloned.1.call-done = bf16[1,2048,2048]{2,1,0:T(8,128)(2,1)} async-done(((bf16[1,256,2048]{2,1,0:T(8,128)(2,1)}), bf16[1,2048,2048]{2,1,0:T(8,128)(2,1)}) %all-gather.17.cloned.1.call-update) | async-done | bytes 8388624 | tf_op jit(solution)/shard_map/all_gather | solution.py:74
  420.5 12.3 %copy.21 = bf16[1,2048,2048]{1,2,0:T(8,128)(2,1)} copy(bf16[1,2048,2048]{2,1,0:T(8,128)(2,1)} %all-gather.17.cloned.1.call-done) | data formatting | bytes 16777216 | tf_op jit(solution)/shard_map/all_gather | solution.py:74
  432.8 160.1 %all-gather.19.cloned.1.call-done = bf16[1,2048,2048]{1,2,0:T(8,128)(2,1)} async-done(((bf16[1,256,2048]{1,2,0:T(8,128)(2,1)}), bf16[1,2048,2048]{1,2,0:T(8,128)(2,1)}) %all-gather.19.cloned.1.call-update) | async-done | bytes 8388624 | tf_op jit(solution)/shard_map/all_gather | solution.py:77
  592.9 18.5 %fusion.2 = (f32[16,256]{1,0:T(8,128)S(1)}, f32[16,2048,256]{1,2,0:T(8,128)}) fusion(pred[256,2048]{1,0:T(8,128)(4,1)S(1)} %convolution_compare_fusion, bf16[2048,16,128]{0,2,1:T(8,128)(2,1)} %bitcast.123, bf16[256,16,128]{2,1,0:T(8,128)(2,1)S(1)} %bitcast.120), kind=kOutput, calls=%fused_computation.8 | convolution fusion | flops 2172645376 | bytes 43532288 | tf_op jit(solution)/shard_map/qhd,khd->hqk/dot_general | solution.py:32
  611.4 153.9 %all-gather.15.cloned.1.call-done = bf16[1,2048,2048]{1,2,0:T(8,128)(2,1)} async-done(((bf16[1,256,2048]{1,2,0:T(8,128)(2,1)}), bf16[1,2048,2048]{1,2,0:T(8,128)(2,1)}) %all-gather.15.cloned.1.call-update) | async-done | bytes 8388624 | tf_op jit(solution)/shard_map/all_gather | solution.py:73
  765.3 18.5 %fusion = (f32[16,256]{1,0:T(8,128)S(1)}, f32[16,256,2048]{2,1,0:T(8,128)}) fusion(pred[256,2048]{1,0:T(8,128)(4,1)S(1)} %convolution_compare_fusion.2, bf16[2048,16,128]{0,2,1:T(8,128)(2,1)} %bitcast.124, bf16[256,16,128]{2,1,0:T(8,128)(2,1)S(1)} %bitcast.121), kind=kOutput, calls=%fused_computation.6 | convolution fusion | flops 2172645376 | bytes 43532288 | tf_op jit(solution)/shard_map/qhd,khd->hqk/dot_general | solution.py:32
  783.8 153.9 %all-gather.11.cloned.1.call-done = bf16[2048,2048]{0,1:T(8,128)(2,1)} async-done(((bf16[256,2048]{0,1:T(8,128)(2,1)}), bf16[2048,2048]{0,1:T(8,128)(2,1)}) %all-gather.11.cloned.1.call-update) | async-done | bytes 8388624 | tf_op jit(solution)/shard_map/all_gather | solution.py:75
  937.7 18.5 %fusion.1 = (f32[16,256]{1,0:T(8,128)S(1)}, f32[16,2048,256]{1,2,0:T(8,128)}) fusion(pred[256,2048]{1,0:T(8,128)(4,1)S(1)} %convolution_compare_fusion.1, bf16[2048,16,128]{0,2,1:T(8,128)(2,1)} %bitcast.125, bf16[256,16,128]{2,1,0:T(8,128)(2,1)S(1)} %bitcast.122), kind=kOutput, calls=%fused_computation.7 | convolution fusion | flops 2172645376 | bytes 43532288 | tf_op jit(solution)/shard_map/qhd,khd->hqk/dot_general | solution.py:32
  956.3 0.0 slice-start
  956.3 0.0 slice-start.1
  956.3 17.0 %fusion.7 = f32[16,256]{1,0:T(8,128)S(1)} fusion(f32[16,2048,256]{1,2,0:T(8,128)} %get-tuple-element.15, f32[16,256]{1,0:T(8,128)S(1)} %get-tuple-element.9, pred[256,2048]{1,0:T(8,128)(4,1)S(1)} %convolution_compare_fusion), kind=kLoop, calls=%fused_computation.13 | loop fusion | flops 41938944 | bytes 34111488 | tf_op jit(solution)/shard_map/reduce_sum | solution.py:39
  973.3 0.0 slice-done
  973.3 0.0 slice-done.1
  973.3 15.7 %fusion.9 = f32[16,128,256]{2,1,0:T(8,128)} fusion(bf16[2048,16,128]{0,2,1:T(8,128)(2,1)S(1)} %bitcast.129, f32[16,2048,256]{1,2,0:T(8,128)} %get-tuple-element.15, f32[16,256]{1,0:T(8,128)S(1)} %get-tuple-element.9, pred[256,2048]{1,0:T(8,128)(4,1)S(1)} %convolution_compare_fusion), kind=kOutput, calls=%fused_computation.15 | convolution fusion | flops 2189426688 | bytes 44580864 | tf_op jit(solution)/shard_map/hqk,khd->qhd/dot_general | solution.py:40
  989.0 121.2 %all-gather.13.cloned.1.call-done = bf16[2048,2048]{0,1:T(8,128)(2,1)} async-done(((bf16[256,2048]{0,1:T(8,128)(2,1)}), bf16[2048,2048]{0,1:T(8,128)(2,1)}) %all-gather.13.cloned.1.call-update) | async-done | bytes 8388624 | tf_op jit(solution)/shard_map/all_gather | solution.py:76
  1110.2 18.2 %fusion.11 = f32[16,128,256]{2,1,0:T(8,128)} fusion(bf16[2048,16,128]{0,2,1:T(8,128)(2,1)} %bitcast.132, f32[16,2048,256]{1,2,0:T(8,128)} %get-tuple-element.17, f32[16,256]{1,0:T(8,128)S(1)} %get-tuple-element.10, pred[256,2048]{1,0:T(8,128)(4,1)S(1)} %convolution_compare_fusion.1), kind=kOutput, calls=%fused_computation.16 | convolution fusion | flops 2189426688 | bytes 44580864 | tf_op jit(solution)/shard_map/hqk,khd->qhd/dot_general | solution.py:40
  1128.4 26.2 %fusion.3 = (f32[16,256]{1,0:T(8,128)S(1)}, f32[16,256]{1,0:T(8,128)S(1)}) fusion(f32[16,256,2048]{2,1,0:T(8,128)} %get-tuple-element.19, f32[16,256]{1,0:T(8,128)S(1)} %get-tuple-element.13, pred[256,2048]{1,0:T(8,128)(4,1)S(1)} %convolution_compare_fusion.2, f32[16,256]{1,0:T(8,128)S(1)} %get-tuple-element.10, f32[16,2048,256]{1,2,0:T(8,128)} %get-tuple-element.17, ...), kind=kLoop, calls=%fused_computation.9 | loop fusion | flops 83877888 | bytes 68222976 | tf_op jit(solution)/shard_map/reduce_sum | solution.py:39
  1154.6 18.6 %fusion.20 = bf16[256,16,128]{0,2,1:T(8,128)(2,1)S(1)} fusion(f32[16,128,256]{2,1,0:T(8,128)} %fusion.9, f32[16,128,256]{2,1,0:T(8,128)} %fusion.11, bf16[2048,16,128]{0,2,1:T(8,128)(2,1)} %bitcast.126, f32[16,256,2048]{2,1,0:T(8,128)} %get-tuple-element.19, f32[16,256]{1,0:T(8,128)S(1)} %get-tuple-element.13, ...), kind=kOutput, calls=%fused_computation.28 | convolution fusion | flops 2193096704 | bytes 47792128 | tf_op jit(solution)/shard_map/hqk,khd->qhd/dot_general | solution.py:40
  1173.2 0.6 copy.32
  1173.9 0.0 collective-permute-done
  1173.9 2.6 fusion.25
  (7 shorter events, 0.1 us)
Async XLA Ops:
  7.4 106.9 %all-reduce.3.cloned.1.call-start = ((), (), s32[]{:S(2)}) async-start(), calls=%async_computation.6 | async-start | bytes 4194304 | tf_op jit(solution)/shard_map/psum | solution.py:19
  8.9 10.4 copy-start
  12.9 175.8 %all-gather.21.cloned.1.call-start = ((), (), s32[]{:S(2)}) async-start(), calls=%async_computation.5 | async-start | bytes 9437184 | tf_op jit(solution)/shard_map/all_gather | solution.py:78
  15.9 404.6 %all-gather.17.cloned.1.call-start = ((), (), s32[]{:S(2)}) async-start(), calls=%async_computation.3 | async-start | bytes 9437184 | tf_op jit(solution)/shard_map/all_gather | solution.py:74
  16.5 576.4 %all-gather.19.cloned.1.call-start = ((), (), s32[]{:S(2)}) async-start(), calls=%async_computation.4 | async-start | bytes 9437184 | tf_op jit(solution)/shard_map/all_gather | solution.py:77
  19.2 746.1 %all-gather.15.cloned.1.call-start = ((), (), s32[]{:S(2)}) async-start(), calls=%async_computation.2 | async-start | bytes 9437184 | tf_op jit(solution)/shard_map/all_gather | solution.py:73
  19.9 917.8 %all-gather.11.cloned.1.call-start = ((), (), s32[]{:S(2)}) async-start(), calls=%async_computation | async-start | bytes 9437184 | tf_op jit(solution)/shard_map/all_gather | solution.py:75
  114.3 995.9 %all-gather.13.cloned.1.call-start = ((), (), s32[]{:S(2)}) async-start(), calls=%async_computation.1 | async-start | bytes 9437184 | tf_op jit(solution)/shard_map/all_gather | solution.py:76
  114.4 1059.5 %collective-permute-start = (bf16[1,256,2048]{2,1,0:T(8,128)(2,1)}, bf16[1,256,2048]{2,1,0:T(8,128)(2,1)}, u32[]{:S(2)}, u32[]{:S(2)}) collective-permute-start(bf16[1,256,2048]{2,1,0:T(8,128)(2,1)} %param.8), channel_id=1, source_target_pairs={{0,16},{16,32},{32,48},{48,64},{64,80},{80,96},{96,112},{1,17},{17... | collective-permute-start | bytes 3145736 | tf_op jit(solution)/shard_map/ppermute | solution.py:14
  956.3 17.0 %slice-start = ((s8[8388608]{0:T(1024)(128)(4,1)}), s8[4194304]{0:T(1024)(128)(4,1)S(1)}, s32[]{:S(2)}) async-start(s8[8388608]{0:T(1024)(128)(4,1)} %bitcast.127), calls=%async_computation.7 | async-start | bytes 8388608
  956.3 17.0 %slice-start.1 = ((s8[8388608]{0:T(1024)(128)(4,1)}), s8[4194304]{0:T(1024)(128)(4,1)S(1)}, s32[]{:S(2)}) async-start(s8[8388608]{0:T(1024)(128)(4,1)} %bitcast.127), calls=%async_computation.8 | async-start | bytes 8388608
Sparse Core Ops, SparseCore 0:
  13.0 101.2 all-reduce.2
Sparse Core Ops, SparseCore 1:
  16.0 172.7 all-gather.20
  190.2 230.2 all-gather.16
  421.9 170.9 all-gather.18
  594.5 170.8 all-gather.14
  766.9 170.8 all-gather.10
  939.3 170.8 all-gather.12
where the time goes:
time: 1190 us; the launch traced here: 1180 us
  waiting for transfers between devices  969 us (81%)
  matrix products  112 us (9%)
  other arithmetic  47.9 us (4%)
  local copies, waits for them, and re-layouts  35 us (3%)
  between operations  15.8 us (1%)
    all_gather x1, waiting for transfers between devices, body(): lax.all_gather(span_v[0], 'seq', axis=0, tiled=True)  219 us
    all_gather x1, waiting for transfers between devices, body(): lax.all_gather(cached_k, 'seq', axis=0, tiled=True)  160 us
    all_gather x1, waiting for transfers between devices, body(): lax.all_gather(fresh_k, 'seq', axis=0, tiled=True)  154 us
    all_gather x1, waiting for transfers between devices, body(): lax.all_gather(span_k[0], 'seq', axis=0, tiled=True)  154 us
    all_gather x1, waiting for transfers between devices, body(): lax.all_gather(fresh_v, 'seq', axis=0, tiled=True)  121 us
    psum x1, waiting for transfers between devices, spread(): return lax.psum(block, axis)  94.3 us
    all_gather x1, waiting for transfers between devices, body(): lax.all_gather(cached_v, 'seq', axis=0, tiled=True)  65.2 us
    dot_general x3, matrix products, absorb(): jnp.einsum('qhd,khd->hqk', queries, key_heads, preferred_element_type=jnp...  55.6 us
  transfers between devices with their start and end apart: 8, of which 7 were waited for; matrix products, arithmetic and copies ran while one was open for 16% of the time, Pallas kernels for 0%

commit v1 on v0

--- a/solution.py
+++ b/solution.py
@@ -16,7 +16,7 @@
 
 def spread(block, axis, holder):
     block = jnp.where(lax.axis_index(axis) == holder, block, jnp.zeros_like(block))
-    return lax.psum(block, axis)
+    return jnp.sum(lax.all_gather(block, axis), axis=0)
 
 
 def one_hot_rows(ids, count):

time: 1190 us -> 1370 us (1.15)
  waiting for transfers between devices: 969 us -> 1120 us
  local copies, waits for them, and re-layouts: 35 us -> 57.2 us
    all_gather x0 -> x2, waiting for transfers between devices: none -> 214 us  [spread(): return jnp.sum(lax.all_gather(block, axis), axis=0)]
    all_gather x1, waiting for transfers between devices: 65.2 us -> 162 us  [body(): lax.all_gather(cached_v, 'seq', axis=0, tiled=True)]
    psum x1 -> x0, waiting for transfers between devices: 94.3 us -> none  [spread(): return lax.psum(block, axis)]
    all_gather x1, waiting for transfers between devices: 219 us -> 163 us  [body(): lax.all_gather(span_v[0], 'seq', axis=0, tiled=True)]
    all_gather x0 -> x2, local copies, waits for them, and re-layouts: none -> 24.5 us  [the longest x1 12.3 us: body(): lax.all_gather(fresh_v, 'seq', axis=0, tiled=True)]
  transfers between devices with their start and end apart: 8 -> 9, of which waited for: 7 -> 8; matrix products, arithmetic and copies ran while one was open for 16% -> 16% of each run, Pallas kernels for 0% -> 0%
where the time goes in v1:
time: 1370 us
  waiting for transfers between devices  1120 us (82%)
  matrix products  111 us (8%)
  other arithmetic  60.8 us (4%)
  local copies, waits for them, and re-layouts  57.2 us (4%)
  between operations  14.3 us (1%)
    all_gather x2, waiting for transfers between devices, spread(): return jnp.sum(lax.all_gather(block, axis), axis=0)  214 us
    all_gather x1, waiting for transfers between devices, body(): lax.all_gather(span_v[0], 'seq', axis=0, tiled=True)  163 us
    all_gather x1, waiting for transfers between devices, body(): lax.all_gather(cached_k, 'seq', axis=0, tiled=True)  163 us
    all_gather x1, waiting for transfers between devices, body(): lax.all_gather(cached_v, 'seq', axis=0, tiled=True)  162 us
    all_gather x1, waiting for transfers between devices, body(): lax.all_gather(fresh_k, 'seq', axis=0, tiled=True)  155 us
    all_gather x1, waiting for transfers between devices, body(): lax.all_gather(span_k[0], 'seq', axis=0, tiled=True)  154 us
    all_gather x1, waiting for transfers between devices, body(): lax.all_gather(fresh_v, 'seq', axis=0, tiled=True)  112 us
    dot_general x3, matrix products, absorb(): jnp.einsum('qhd,khd->hqk', queries, key_heads, preferred_element_type=jnp...  55.6 us
  transfers between devices with their start and end apart: 9, of which 8 were waited for; matrix products, arithmetic and copies ran while one was open for 16% of the time, Pallas kernels for 0%

profile of v1, /device:TPU:15, one launch (start us, length us, event | category | flops | bytes accessed | tf_op | source)
XLA Modules:
  0.0 1369.3 jit_solution(16169745638842569647)
XLA Ops:
  6.5 0.0 copy-start
  6.5 0.0 copy-start.1
  6.5 0.0 all-gather.13.cloned.1.call-start
  6.5 1.1 broadcast_select_fusion.1
  7.6 0.0 all-gather.13.cloned.1.call-update
  7.6 0.0 all-gather.17.cloned.1.call-start
  7.7 1.1 broadcast_select_fusion
  8.8 0.0 all-gather.17.cloned.1.call-update
  8.8 0.0 all-gather.27.cloned.1.call-start
  9.5 2.3 constant_dynamic-slice_fusion
  11.8 0.0 all-gather.27.cloned.1.call-update
  11.8 0.0 all-gather.23.cloned.1.call-start
  11.9 0.5 all-gather.23.cloned.1.call-update
  12.4 0.0 all-gather.25.cloned.1.call-start
  12.5 1.3 constant_dynamic-slice_fusion.1
  13.8 1.3 copy.50
  15.1 0.0 all-gather.25.cloned.1.call-update
  15.1 0.0 all-gather.21.cloned.1.call-start
  15.1 2.3 copy.30
  17.4 0.0 all-gather.21.cloned.1.call-update
  17.4 0.0 all-gather.15.cloned.1.call-start
  17.5 101.9 %all-gather.13.cloned.1.call-done = bf16[8,256,2048]{2,1,0:T(8,128)(2,1)} async-done(((bf16[1,256,2048]{2,1,0:T(8,128)(2,1)}), bf16[8,256,2048]{2,1,0:T(8,128)(2,1)}) %all-gather.13.cloned.1.call-update) | async-done | bytes 8388624 | tf_op jit(solution)/shard_map/all_gather | solution.py:19
  119.3 6.4 reduce_sum.57
  125.7 0.0 all-gather.15.cloned.1.call-update
  125.8 0.0 all-gather.19.cloned.1.call-start
  125.8 3.0 collective-permute-start
  128.9 112.4 %all-gather.17.cloned.1.call-done = bf16[8,256,2048]{2,1,0:T(8,128)(2,1)} async-done(((bf16[1,256,2048]{2,1,0:T(8,128)(2,1)}), bf16[8,256,2048]{2,1,0:T(8,128)(2,1)}) %all-gather.17.cloned.1.call-update) | async-done | bytes 8388624 | tf_op jit(solution)/shard_map/all_gather | solution.py:19
  241.2 6.4 reduce_sum.58
  247.6 0.0 all-gather.19.cloned.1.call-update
  247.7 0.0 copy-done
  247.7 0.2 copy.51
  247.9 0.0 copy-done.1
  247.9 0.2 fusion.35
  248.2 1.0 convolution_compare_fusion
  249.2 1.0 convolution_compare_fusion.1
  250.1 1.0 convolution_compare_fusion.2
  251.1 161.7 %all-gather.27.cloned.1.call-done = bf16[1,2048,2048]{2,1,0:T(8,128)(2,1)} async-done(((bf16[1,256,2048]{2,1,0:T(8,128)(2,1)}), bf16[1,2048,2048]{2,1,0:T(8,128)(2,1)}) %all-gather.27.cloned.1.call-update) | async-done | bytes 8388624 | tf_op jit(solution)/shard_map/all_gather | solution.py:78
  412.8 12.3 copy.43
  425.1 163.0 %all-gather.23.cloned.1.call-done = bf16[1,2048,2048]{2,1,0:T(8,128)(2,1)} async-done(((bf16[1,256,2048]{2,1,0:T(8,128)(2,1)}), bf16[1,2048,2048]{2,1,0:T(8,128)(2,1)}) %all-gather.23.cloned.1.call-update) | async-done | bytes 8388624 | tf_op jit(solution)/shard_map/all_gather | solution.py:74
  588.1 12.3 copy.33
  600.4 162.5 %all-gather.25.cloned.1.call-done = bf16[1,2048,2048]{1,2,0:T(8,128)(2,1)} async-done(((bf16[1,256,2048]{1,2,0:T(8,128)(2,1)}), bf16[1,2048,2048]{1,2,0:T(8,128)(2,1)}) %all-gather.25.cloned.1.call-update) | async-done | bytes 8388624 | tf_op jit(solution)/shard_map/all_gather | solution.py:77
  762.9 18.5 %fusion.2 = (f32[16,256]{1,0:T(8,128)S(1)}, f32[16,2048,256]{1,2,0:T(8,128)}) fusion(pred[256,2048]{1,0:T(8,128)(4,1)S(1)} %convolution_compare_fusion, bf16[2048,16,128]{0,2,1:T(8,128)(2,1)} %bitcast.120, bf16[256,16,128]{2,1,0:T(8,128)(2,1)S(1)} %bitcast.117), kind=kOutput, calls=%fused_computation.8 | convolution fusion | flops 2172645376 | bytes 43532288 | tf_op jit(solution)/shard_map/qhd,khd->hqk/dot_general | solution.py:32
  781.4 153.9 %all-gather.21.cloned.1.call-done = bf16[1,2048,2048]{1,2,0:T(8,128)(2,1)} async-done(((bf16[1,256,2048]{1,2,0:T(8,128)(2,1)}), bf16[1,2048,2048]{1,2,0:T(8,128)(2,1)}) %all-gather.21.cloned.1.call-update) | async-done | bytes 8388624 | tf_op jit(solution)/shard_map/all_gather | solution.py:73
  935.4 18.5 %fusion = (f32[16,256]{1,0:T(8,128)S(1)}, f32[16,256,2048]{2,1,0:T(8,128)}) fusion(pred[256,2048]{1,0:T(8,128)(4,1)S(1)} %convolution_compare_fusion.2, bf16[2048,16,128]{0,2,1:T(8,128)(2,1)} %bitcast.121, bf16[256,16,128]{2,1,0:T(8,128)(2,1)S(1)} %bitcast.118), kind=kOutput, calls=%fused_computation.6 | convolution fusion | flops 2172645376 | bytes 43532288 | tf_op jit(solution)/shard_map/qhd,khd->hqk/dot_general | solution.py:32
  953.8 154.5 %all-gather.15.cloned.1.call-done = bf16[2048,2048]{1,0:T(8,128)(2,1)} async-done(((bf16[256,2048]{1,0:T(8,128)(2,1)}), bf16[2048,2048]{1,0:T(8,128)(2,1)}) %all-gather.15.cloned.1.call-update) | async-done | bytes 8388624 | tf_op jit(solution)/shard_map/all_gather | solution.py:75
  1108.4 12.2 copy.34
  1120.5 18.6 %fusion.1 = (f32[16,256]{1,0:T(8,128)S(1)}, f32[16,2048,256]{1,2,0:T(8,128)}) fusion(pred[256,2048]{1,0:T(8,128)(4,1)S(1)} %convolution_compare_fusion.1, bf16[2048,16,128]{0,2,1:T(8,128)(2,1)} %bitcast.116, bf16[256,16,128]{2,1,0:T(8,128)(2,1)S(1)} %bitcast.119), kind=kOutput, calls=%fused_computation.7 | convolution fusion | flops 2172645376 | bytes 43532288 | tf_op jit(solution)/shard_map/qhd,khd->hqk/dot_general | solution.py:32
  1139.2 0.0 slice-start
  1139.2 0.0 slice-start.1
  1139.2 16.9 %fusion.7 = f32[16,256]{1,0:T(8,128)S(1)} fusion(f32[16,2048,256]{1,2,0:T(8,128)} %get-tuple-element.13, f32[16,256]{1,0:T(8,128)S(1)} %get-tuple-element.7, pred[256,2048]{1,0:T(8,128)(4,1)S(1)} %convolution_compare_fusion), kind=kLoop, calls=%fused_computation.13 | loop fusion | flops 41938944 | bytes 34111488 | tf_op jit(solution)/shard_map/reduce_sum | solution.py:39
  1156.1 0.0 slice-done
  1156.1 0.0 slice-done.1
  1156.2 15.6 %fusion.9 = f32[16,128,256]{2,1,0:T(8,128)} fusion(bf16[2048,16,128]{0,2,1:T(8,128)(2,1)S(1)} %bitcast.125, f32[16,2048,256]{1,2,0:T(8,128)} %get-tuple-element.13, f32[16,256]{1,0:T(8,128)S(1)} %get-tuple-element.7, pred[256,2048]{1,0:T(8,128)(4,1)S(1)} %convolution_compare_fusion), kind=kOutput, calls=%fused_computation.15 | convolution fusion | flops 2189426688 | bytes 44580864 | tf_op jit(solution)/shard_map/hqk,khd->qhd/dot_general | solution.py:40
  1171.8 112.0 %all-gather.19.cloned.1.call-done = bf16[2048,2048]{1,0:T(8,128)(2,1)} async-done(((bf16[256,2048]{1,0:T(8,128)(2,1)}), bf16[2048,2048]{1,0:T(8,128)(2,1)}) %all-gather.19.cloned.1.call-update) | async-done | bytes 8388624 | tf_op jit(solution)/shard_map/all_gather | solution.py:76
  1283.8 12.3 copy.38
  1296.1 18.3 %fusion.11 = f32[16,128,256]{2,1,0:T(8,128)} fusion(bf16[2048,16,128]{0,2,1:T(8,128)(2,1)} %bitcast.126, f32[16,2048,256]{1,2,0:T(8,128)} %get-tuple-element.15, f32[16,256]{1,0:T(8,128)S(1)} %get-tuple-element.8, pred[256,2048]{1,0:T(8,128)(4,1)S(1)} %convolution_compare_fusion.1), kind=kOutput, calls=%fused_computation.16 | convolution fusion | flops 2189426688 | bytes 44580864 | tf_op jit(solution)/shard_map/hqk,khd->qhd/dot_general | solution.py:40
  1314.4 26.2 %fusion.3 = (f32[16,256]{1,0:T(8,128)S(1)}, f32[16,256]{1,0:T(8,128)S(1)}) fusion(f32[16,256,2048]{2,1,0:T(8,128)} %get-tuple-element.17, f32[16,256]{1,0:T(8,128)S(1)} %get-tuple-element.11, pred[256,2048]{1,0:T(8,128)(4,1)S(1)} %convolution_compare_fusion.2, f32[16,256]{1,0:T(8,128)S(1)} %get-tuple-element.8, f32[16,2048,256]{1,2,0:T(8,128)} %get-tuple-element.15, ...), kind=kLoop, calls=%fused_computation.9 | loop fusion | flops 83877888 | bytes 68222976 | tf_op jit(solution)/shard_map/reduce_sum | solution.py:39
  1340.7 18.6 %fusion.20 = bf16[256,16,128]{0,2,1:T(8,128)(2,1)S(1)} fusion(f32[16,128,256]{2,1,0:T(8,128)} %fusion.9, f32[16,128,256]{2,1,0:T(8,128)} %fusion.11, bf16[2048,16,128]{0,2,1:T(8,128)(2,1)} %bitcast.122, f32[16,256,2048]{2,1,0:T(8,128)} %get-tuple-element.17, f32[16,256]{1,0:T(8,128)S(1)} %get-tuple-element.11, ...), kind=kOutput, calls=%fused_computation.28 | convolution fusion | flops 2193096704 | bytes 47792128 | tf_op jit(solution)/shard_map/hqk,khd->qhd/dot_general | solution.py:40
  1359.2 0.6 copy.44
  1359.9 0.0 collective-permute-done
  1359.9 2.6 fusion.25
  (7 shorter events, 0.1 us)
Async XLA Ops:
  6.5 241.2 %copy-start = (bf16[1,256,2048]{2,1,0:T(8,128)(2,1)S(1)}, bf16[1,256,2048]{2,1,0:T(8,128)(2,1)}, u32[]{:S(2)}) copy-start(bf16[1,256,2048]{2,1,0:T(8,128)(2,1)} %param.9) | copy-start | bytes 3145732
  6.5 241.4 %copy-start.1 = (s32[1,16,48]{2,1,0:T(8,128)S(1)}, s32[1,16,48]{2,1,0:T(8,128)}, u32[]{:S(2)}) copy-start(s32[1,16,48]{2,1,0:T(8,128)} %param.15) | copy-start | bytes 9220
  6.5 112.8 %all-gather.13.cloned.1.call-start = ((), (), s32[]{:S(2)}) async-start(), calls=%async_computation | async-start | bytes 9437184 | tf_op jit(solution)/shard_map/all_gather | solution.py:19
  7.6 233.6 %all-gather.17.cloned.1.call-start = ((), (), s32[]{:S(2)}) async-start(), calls=%async_computation.2 | async-start | bytes 9437184 | tf_op jit(solution)/shard_map/all_gather | solution.py:19
  8.8 404.0 %all-gather.27.cloned.1.call-start = ((), (), s32[]{:S(2)}) async-start(), calls=%async_computation.7 | async-start | bytes 9437184 | tf_op jit(solution)/shard_map/all_gather | solution.py:78
  11.8 576.2 %all-gather.23.cloned.1.call-start = ((), (), s32[]{:S(2)}) async-start(), calls=%async_computation.5 | async-start | bytes 9437184 | tf_op jit(solution)/shard_map/all_gather | solution.py:74
  12.4 750.5 %all-gather.25.cloned.1.call-start = ((), (), s32[]{:S(2)}) async-start(), calls=%async_computation.6 | async-start | bytes 9437184 | tf_op jit(solution)/shard_map/all_gather | solution.py:77
  15.1 920.3 %all-gather.21.cloned.1.call-start = ((), (), s32[]{:S(2)}) async-start(), calls=%async_computation.4 | async-start | bytes 9437184 | tf_op jit(solution)/shard_map/all_gather | solution.py:73
  17.4 1091.0 %all-gather.15.cloned.1.call-start = ((), (), s32[]{:S(2)}) async-start(), calls=%async_computation.1 | async-start | bytes 9437184 | tf_op jit(solution)/shard_map/all_gather | solution.py:75
  125.8 1158.0 %all-gather.19.cloned.1.call-start = ((), (), s32[]{:S(2)}) async-start(), calls=%async_computation.3 | async-start | bytes 9437184 | tf_op jit(solution)/shard_map/all_gather | solution.py:76
  125.8 1234.1 %collective-permute-start = (bf16[1,256,2048]{2,1,0:T(8,128)(2,1)}, bf16[1,256,2048]{2,1,0:T(8,128)(2,1)}, u32[]{:S(2)}, u32[]{:S(2)}) collective-permute-start(bf16[1,256,2048]{2,1,0:T(8,128)(2,1)} %param.8), channel_id=1, source_target_pairs={{0,16},{16,32},{32,48},{48,64},{64,80},{80,96},{96,112},{1,17},{17... | collective-permute-start | bytes 3145736 | tf_op jit(solution)/shard_map/ppermute | solution.py:14
  1139.2 17.0 %slice-start = ((s8[8388608]{0:T(1024)(128)(4,1)}), s8[4194304]{0:T(1024)(128)(4,1)S(1)}, s32[]{:S(2)}) async-start(s8[8388608]{0:T(1024)(128)(4,1)} %bitcast.123), calls=%async_computation.8 | async-start | bytes 8388608
  1139.2 17.0 %slice-start.1 = ((s8[8388608]{0:T(1024)(128)(4,1)}), s8[4194304]{0:T(1024)(128)(4,1)S(1)}, s32[]{:S(2)}) async-start(s8[8388608]{0:T(1024)(128)(4,1)} %bitcast.123), calls=%async_computation.9 | async-start | bytes 8388608
Sparse Core Ops, SparseCore 0:
  9.7 109.5 all-gather.12
  121.7 119.5 all-gather.16
  242.9 169.8 all-gather.26
  414.3 173.7 all-gather.22
  589.5 173.3 all-gather.24
  764.3 170.9 all-gather.20
  937.0 171.3 all-gather.14
  1110.0 173.7 all-gather.18
